TPU v7x, 32 devices: a whole 2x2x4 slice. The times are simulated.
32 devices in a mesh: row: 2 (over y), col: 4 (over x, core), band: 4 (over z).
Axes of the slice: x: 2, y: 2, z: 4, core: 2. Of those that a mesh axis runs over, the one named last changes fastest.
Arguments:
- vis: bfloat16 [64, 4, 2, 512, 512], P('band', None, None, 'row', 'col'), may hold values from -200 to 200
- flags: int32 [64, 4, 512], P('band'), may hold values 0 or 1
- positions: float32 [4, 3, 512], replicated, may hold values from -4 to 4
- lmn: float32 [3, 8], replicated, may hold values from -3 to 3
- flux: float32 [64, 8], P('band'), may hold values from 0.5 to 2
- gains: float32 [64, 4, 2, 8, 512], P('band', None, None, None, ('row', 'col')), may hold values from -6 to 6
- duals: float32 [64, 4, 2, 8, 512], P('band', None, None, None, ('row', 'col')), may hold values from -2 to 2
Outputs:
- gains_out: float32 [64, 4, 2, 8, 512], P('band', None, None, None, ('row', 'col'))
- duals_out: float32 [64, 4, 2, 8, 512], P('band', None, None, None, ('row', 'col'))
All inputs are finite; a program needn't handle non-finite values. No bound on the sum of `flags` on one device may be relied on, other than what follows from the above.
Results may differ from a plain program's by a relative error of at most 0.0003.
Values sent between devices are 32-bit elements; how exact they have to be, the bound alone decides.
No kernel may reach another device: no remote copies, remote signals or barrier semaphores. Data moves between devices by JAX's collectives and lax.ppermute only.
A program may use at most 128 MiB of HBM per device.

v0:
```python
import math
import jax
import jax.numpy as jnp
from jax import lax
from jax.sharding import PartitionSpec as P

S = 512
F = 64
ITERS = 2
PENALTY = 0.05
HIGH = lax.Precision.HIGHEST


def basis(count):
    grid = 2.0 * jnp.arange(count, dtype=jnp.float32) / (count - 1) - 1.0
    return jnp.stack([grid**power for power in range(4)], axis=1)


def rotate(positions, lmn, freq):
    geometry = jnp.einsum("tks,kd->tds", positions, lmn, precision=HIGH)
    angle = 2.0 * math.pi * freq[:, None, None, None] * geometry[None]
    return (jnp.cos(angle), -jnp.sin(angle))


def complex_mul(a_re, a_im, b_re, b_im):
    return (a_re * b_re - a_im * b_im, a_re * b_im + a_im * b_re)


def solve_fit(rhs):
    full = basis(F)
    gram = jnp.dot(full.T, full, precision=HIGH)
    factor = jnp.linalg.cholesky(gram)
    flat = rhs.reshape(rhs.shape[0], -1)
    return jax.scipy.linalg.cho_solve((factor, True), flat).reshape(rhs.shape)


def shards(vis, flags, positions, lmn, flux, gains, duals):
    width = gains.shape[0]
    first = lax.axis_index("band") * width
    local_basis = lax.dynamic_slice_in_dim(basis(F), first, width, 0)
    freq = 1.0 + (first + jnp.arange(width, dtype=jnp.int32)).astype(jnp.float32) / F
    row_index = lax.axis_index("row")
    col_index = lax.axis_index("col")
    row_count = vis.shape[3]
    col_count = vis.shape[4]
    owned = gains.shape[4]
    own_start = (row_index * lax.axis_size("col") + col_index) * owned
    row_start = row_index * row_count
    col_start = col_index * col_count
    own_cos, own_sin = rotate(lax.dynamic_slice_in_dim(positions, own_start, owned, 2), lmn, freq)
    row_cos, row_sin = rotate(
        lax.dynamic_slice_in_dim(positions, row_start, row_count, 2), lmn, freq
    )
    col_cos, col_sin = rotate(
        lax.dynamic_slice_in_dim(positions, col_start, col_count, 2), lmn, freq
    )
    all_live = flags.astype(jnp.float32)
    row_live = lax.dynamic_slice_in_dim(all_live, row_start, row_count, 2)
    col_live = lax.dynamic_slice_in_dim(all_live, col_start, col_count, 2)
    own_live = lax.dynamic_slice_in_dim(all_live, own_start, owned, 2)
    row_ids = row_start + jnp.arange(row_count, dtype=jnp.int32)
    col_ids = col_start + jnp.arange(col_count, dtype=jnp.int32)
    distinct = (row_ids[:, None] != col_ids[None, :]).astype(jnp.float32)
    weight = row_live[:, :, :, None] * col_live[:, :, None, :] * distinct
    vis_re = vis[:, :, 0].astype(jnp.float32)
    vis_im = vis[:, :, 1].astype(jnp.float32)
    scale = flux[:, None, :, None]

    def fit(gain, dual):
        rhs = jnp.einsum("fk,ftcds->ktcds", local_basis, gain + dual, precision=HIGH)
        return solve_fit(lax.psum(rhs, "band"))

    gain, dual = (gains, duals)
    coeffs = fit(gain, dual)
    for step in range(ITERS):
        target = jnp.einsum("fk,ktcds->ftcds", local_basis, coeffs, precision=HIGH) - dual
        every = lax.all_gather(gain, ("row", "col"), axis=4, tiled=True)
        row_gain = lax.dynamic_slice_in_dim(every, row_start, row_count, 4)
        col_gain = lax.dynamic_slice_in_dim(every, col_start, col_count, 4)
        row_re, row_im = complex_mul(row_gain[:, :, 0], row_gain[:, :, 1], row_cos, row_sin)
        col_re, col_im = complex_mul(col_gain[:, :, 0], col_gain[:, :, 1], col_cos, col_sin)
        col_re = scale * col_re
        col_im = scale * col_im
        model_re = jnp.einsum("ftdp,ftdq->ftpq", row_re, col_re, precision=HIGH) + jnp.einsum(
            "ftdp,ftdq->ftpq", row_im, col_im, precision=HIGH
        )
        model_im = jnp.einsum("ftdp,ftdq->ftpq", row_im, col_re, precision=HIGH) - jnp.einsum(
            "ftdp,ftdq->ftpq", row_re, col_im, precision=HIGH
        )
        resid_re = weight * (vis_re - model_re)
        resid_im = weight * (vis_im - model_im)
        squares, samples = lax.psum(
            (jnp.sum(resid_re * resid_re + resid_im * resid_im), jnp.sum(weight)),
            ("row", "col", "band"),
        )
        sum_re = jnp.einsum("ftpq,ftdq->ftdp", resid_re, col_re, precision=HIGH) - jnp.einsum(
            "ftpq,ftdq->ftdp", resid_im, col_im, precision=HIGH
        )
        sum_im = jnp.einsum("ftpq,ftdq->ftdp", resid_re, col_im, precision=HIGH) + jnp.einsum(
            "ftpq,ftdq->ftdp", resid_im, col_re, precision=HIGH
        )
        pairs = lax.psum_scatter(
            jnp.stack([sum_re, sum_im], axis=2), "col", scatter_dimension=4, tiled=True
        )
        every_mag = every[:, :, 0] * every[:, :, 0] + every[:, :, 1] * every[:, :, 1]
        total_mag = jnp.einsum("ftds,fts->ftd", every_mag, all_live, precision=HIGH)
        own_mag = gain[:, :, 0] * gain[:, :, 0] + gain[:, :, 1] * gain[:, :, 1]
        own_flag = own_live[:, :, None, :]
        own_denom = (scale * scale * own_flag * (total_mag[:, :, :, None] - own_flag * own_mag))[
            :, :, None
        ]
        num_re, num_im = complex_mul(own_cos, -own_sin, pairs[:, :, 0], pairs[:, :, 1])
        numer = jnp.stack([num_re, num_im], axis=2)
        rho = PENALTY * S * (squares / samples + 1e-06)
        fresh = (numer + own_denom * gain + rho * target) / (own_denom + rho)
        gain = 0.5 * (gain + fresh)
        coeffs = fit(gain, dual)
        dual = dual + gain - jnp.einsum("fk,ktcds->ftcds", local_basis, coeffs, precision=HIGH)
    return (gain, dual)


def solution(mesh):
    return jax.shard_map(
        shards,
        mesh=mesh,
        in_specs=(
            P("band", None, None, "row", "col"),
            P("band", None, None),
            P(),
            P(),
            P("band", None),
            P("band", None, None, None, ("row", "col")),
            P("band", None, None, None, ("row", "col")),
        ),
        out_specs=(
            P("band", None, None, None, ("row", "col")),
            P("band", None, None, None, ("row", "col")),
        ),
        check_vma=False,
    )
```

profile of v0, /device:TPU:0, one launch (start us, length us, event | category | flops | bytes accessed | tf_op | source)
XLA Modules:
  0.0 711.7 jit_solution(12807473664040143431)
XLA Ops:
  20.6 84.0 %all-gather.3.cloned.1.call-done = f32[16,4,2,8,512]{0,3,2,1,4:T(8,128)} async-done(((f32[16,4,2,8,64]{0,3,2,1,4:T(8,128)}), f32[16,4,2,8,512]{0,3,2,1,4:T(8,128)}) %all-gather.3.cloned.1.call-update) | async-done | bytes 2097168 | tf_op jit(solution)/shard_map/all_gather | solution.py:77
  112.7 7.7 %constant_dynamic-slice_fusion.2 = (f32[16,4,1,8,256]{0,3,2,1,4:T(8,128)}, f32[16,4,1,8,256]{0,3,2,1,4:T(8,128)}) fusion(f32[16,4,2,8,512]{0,3,2,1,4:T(8,128)} %all-gather.3.cloned.1.call-done, s32[]{:T(128)S(6)} %select_n.24, s32[]{:T(128)S(6)} %add.262), kind=kLoop, calls=%fused_computation.128 | loop fusion | bytes 2097160 | tf_op jit(solution)/shard_map/slice | solution.py:80
  129.3 15.9 %fusion.122 = f32[16,4,256,128]{3,2,1,0:T(8,128)S(1)} fusion(f32[16,4,8,128]{3,2,1,0:T(8,128)S(1)} %get-tuple-element.34, f32[16,4,1,8,256]{4,3,1,0,2:T(8,128)S(1)} %copy.197, f32[16,4,1,8,256]{4,3,1,0,2:T(8,128)S(1)} %copy.195, f32[4,8,256]{2,1,0:T(8,128)S(1)} %convolution_bitcast_fusion, f32[16]{0:T(128)S(1)} %add_multiply_fusion), kind=kOutput, calls=%fused_computation.178 | convolution fusion | flops 201981952 | bytes 9732160 | tf_op jit(solution)/shard_map/ftdp,ftdq->ftpq/dot_general | solution.py:84
  145.2 16.0 %fusion.118 = f32[16,4,256,128]{3,2,1,0:T(8,128)S(1)} fusion(f32[16,4,8,128]{3,2,1,0:T(8,128)S(1)} %get-tuple-element.34, f32[16,4,1,8,256]{4,3,1,0,2:T(8,128)S(1)} %copy.197, f32[16,4,1,8,256]{4,3,1,0,2:T(8,128)S(1)} %copy.195, f32[4,8,256]{2,1,0:T(8,128)S(1)} %convolution_bitcast_fusion, f32[16]{0:T(128)S(1)} %add_multiply_fusion), kind=kOutput, calls=%fused_computation.177 | convolution fusion | flops 201981952 | bytes 9732160 | tf_op jit(solution)/shard_map/ftdp,ftdq->ftpq/dot_general | solution.py:87
  161.3 19.2 %fusion = f32[16,4,256,128]{3,2,1,0:T(8,128)S(1)} fusion(f32[16,4,256,128]{3,2,1,0:T(8,128)S(1)} %fusion.122, f32[256,128]{1,0:T(8,128)S(1)} %compare_convert_fusion, f32[16,4,128]{2,1,0:T(4,128)S(1)} %constant_dynamic-slice_fusion.10, f32[16,4,256]{2,1,0:T(4,128)S(1)} %constant_dynamic-slice_fusion.11, bf16[16,4,2,256,128]{4,3,2,1,0:T(8,128)(2,1)S(1)} %bitcast.197, ...), kind=kOutput, calls=%fused_computation.4 | convolution fusion | flops 214564864 | bytes 22544448 | tf_op jit(solution)/shard_map/ftdp,ftdq->ftpq/dot_general | solution.py:84
  180.5 7.2 %fusion.128 = f32[16,4,8,256]{3,2,1,0:T(8,128)S(1)} fusion(f32[16,4,8,128]{3,2,1,0:T(8,128)S(1)} %get-tuple-element.35, f32[16,4,256,128]{3,2,1,0:T(8,128)S(1)} %fusion), kind=kOutput, calls=%fused_computation.182 | convolution fusion | flops 201326592 | bytes 9175040 | tf_op jit(solution)/shard_map/ftpq,ftdq->ftdp/dot_general | solution.py:99
  194.8 20.2 %add_reduce_fusion.1 = (f32[]{:T(128)}, f32[16,4,256,128]{3,2,1,0:T(8,128)S(1)}) fusion(f32[16,4,256,128]{3,2,1,0:T(8,128)S(1)} %fusion, f32[16,4,256,128]{3,2,1,0:T(8,128)S(1)} %fusion.118, f32[16,4,8,128]{3,2,1,0:T(8,128)S(1)} %get-tuple-element.35, f32[16,4,1,8,256]{4,3,1,0,2:T(8,128)S(1)} %copy.197, f32[16,4,1,8,256]{4,3,1,0,2:T(8,128)S(1)} %copy.195, ...), kind=kOutput, calls=%fused_computation.21 | convolution fusion | flops 222953472 | bytes 30933060 | tf_op jit(solution)/shard_map/ftdp,ftdq->ftpq/dot_general | solution.py:87
  222.0 7.3 %fusion.13 = f32[16,4,1,8,256]{4,3,1,0,2:T(8,128)S(1)} fusion(f32[16,4,8,256]{3,2,1,0:T(8,128)S(1)} %fusion.127, f32[16,4,8,128]{3,2,1,0:T(8,128)S(1)} %get-tuple-element.35, f32[16,4,256,128]{3,2,1,0:T(8,128)S(1)} %get-tuple-element.41), kind=kOutput, calls=%fused_computation.30 | convolution fusion | flops 201457664 | bytes 9699328 | tf_op jit(solution)/shard_map/ftpq,ftdq->ftdp/dot_general | solution.py:96
  229.4 12.1 %copy.182 = f32[16,4,2,8,256]{3,1,0,2,4:T(4,128)} copy(f32[16,4,2,8,256]{4,3,1,0,2:T(8,128)S(1)} %pad_maximum_fusion) | data formatting | bytes 2097152
  241.6 22.3 %reshape.149 = f32[256,1024]{1,0:T(8,128)} reshape(f32[256,2,16,4,8]{4,3,2,1,0:T(4,128)} %bitcast.194) | data formatting | bytes 2097152
  270.8 40.1 %all-reduce = (f32[]{:T(128)}, f32[]{:T(128)}) all-reduce(f32[]{:T(128)} %get-tuple-element.40, f32[]{:T(128)} %fusion.12), channel_id=1, replica_groups=mesh['row'=2,'col'=4,'band'=4] {'row','col','band'}, use_global_device_ids=true, to_apply=%region_2.3 | all-reduce | flops 2 | bytes 16 | tf_op jit(solution)/shard_map/psum | solution.py:92
  319.4 7.2 %reshape.150 = f32[64,2,16,4,8]{4,3,2,1,0:T(4,128)} reshape(f32[64,1024]{1,0:T(8,128)} %reduce-scatter.7.cloned.1.call-done) | data formatting | bytes 524288
  346.3 87.7 %all-gather.5.cloned.1.call-done = f32[16,4,2,8,512]{0,3,2,1,4:T(8,128)} async-done(((f32[16,4,2,8,64]{0,3,2,1,4:T(8,128)}), f32[16,4,2,8,512]{0,3,2,1,4:T(8,128)}) %all-gather.5.cloned.1.call-update) | async-done | bytes 2097168 | tf_op jit(solution)/shard_map/all_gather | solution.py:77
  444.1 7.7 %constant_dynamic-slice_fusion.1 = (f32[16,4,1,8,256]{0,3,2,1,4:T(8,128)}, f32[16,4,1,8,256]{0,3,2,1,4:T(8,128)}) fusion(f32[16,4,2,8,512]{0,3,2,1,4:T(8,128)} %all-gather.5.cloned.1.call-done, s32[]{:T(128)S(6)} %select_n.24, s32[]{:T(128)S(6)} %add.262), kind=kLoop, calls=%fused_computation.127 | loop fusion | bytes 2097160 | tf_op jit(solution)/shard_map/slice | solution.py:80
  460.8 15.9 %fusion.116 = f32[16,4,256,128]{3,2,1,0:T(8,128)S(1)} fusion(f32[16,4,8,128]{3,2,1,0:T(8,128)S(1)} %get-tuple-element.33, f32[16,4,1,8,256]{4,3,1,0,2:T(8,128)S(1)} %copy.206, f32[16,4,1,8,256]{4,3,1,0,2:T(8,128)S(1)} %copy.205, f32[4,8,256]{2,1,0:T(8,128)S(1)} %convolution_bitcast_fusion, f32[16]{0:T(128)S(1)} %add_multiply_fusion), kind=kOutput, calls=%fused_computation.176 | convolution fusion | flops 201981952 | bytes 9732160 | tf_op jit(solution)/shard_map/ftdp,ftdq->ftpq/dot_general | solution.py:84
  476.6 16.0 %fusion.112 = f32[16,4,256,128]{3,2,1,0:T(8,128)S(1)} fusion(f32[16,4,8,128]{3,2,1,0:T(8,128)S(1)} %get-tuple-element.33, f32[16,4,1,8,256]{4,3,1,0,2:T(8,128)S(1)} %copy.206, f32[16,4,1,8,256]{4,3,1,0,2:T(8,128)S(1)} %copy.205, f32[4,8,256]{2,1,0:T(8,128)S(1)} %convolution_bitcast_fusion, f32[16]{0:T(128)S(1)} %add_multiply_fusion), kind=kOutput, calls=%fused_computation.175 | convolution fusion | flops 201981952 | bytes 9732160 | tf_op jit(solution)/shard_map/ftdp,ftdq->ftpq/dot_general | solution.py:87
  492.7 19.2 %fusion.1 = f32[16,4,256,128]{3,2,1,0:T(8,128)S(1)} fusion(f32[16,4,256,128]{3,2,1,0:T(8,128)S(1)} %fusion.116, f32[256,128]{1,0:T(8,128)S(1)} %compare_convert_fusion, f32[16,4,128]{2,1,0:T(4,128)S(1)} %constant_dynamic-slice_fusion.10, f32[16,4,256]{2,1,0:T(4,128)S(1)} %constant_dynamic-slice_fusion.11, bf16[16,4,2,256,128]{4,3,2,1,0:T(8,128)(2,1)S(1)} %bitcast.199, ...), kind=kOutput, calls=%fused_computation.5 | convolution fusion | flops 214564864 | bytes 22544448 | tf_op jit(solution)/shard_map/ftdp,ftdq->ftpq/dot_general | solution.py:84
  511.9 7.2 %fusion.131 = f32[16,4,8,256]{3,2,1,0:T(8,128)S(1)} fusion(f32[16,4,8,128]{3,2,1,0:T(8,128)S(1)} %get-tuple-element.32, f32[16,4,256,128]{3,2,1,0:T(8,128)S(1)} %fusion.1), kind=kOutput, calls=%fused_computation.185 | convolution fusion | flops 201326592 | bytes 9175040 | tf_op jit(solution)/shard_map/ftpq,ftdq->ftdp/dot_general | solution.py:99
  526.2 20.2 %add_reduce_fusion = (f32[]{:T(128)}, f32[16,4,256,128]{3,2,1,0:T(8,128)S(1)}) fusion(f32[16,4,256,128]{3,2,1,0:T(8,128)S(1)} %fusion.1, f32[16,4,256,128]{3,2,1,0:T(8,128)S(1)} %fusion.112, f32[16,4,8,128]{3,2,1,0:T(8,128)S(1)} %get-tuple-element.32, f32[16,4,1,8,256]{4,3,1,0,2:T(8,128)S(1)} %copy.206, f32[16,4,1,8,256]{4,3,1,0,2:T(8,128)S(1)} %copy.205, ...), kind=kOutput, calls=%fused_computation.20 | convolution fusion | flops 222953472 | bytes 30933060 | tf_op jit(solution)/shard_map/ftdp,ftdq->ftpq/dot_general | solution.py:87
  553.4 7.3 %fusion.17 = f32[16,4,1,8,256]{4,3,1,0,2:T(8,128)S(1)} fusion(f32[16,4,8,256]{3,2,1,0:T(8,128)S(1)} %fusion.130, f32[16,4,8,128]{3,2,1,0:T(8,128)S(1)} %get-tuple-element.32, f32[16,4,256,128]{3,2,1,0:T(8,128)S(1)} %get-tuple-element.45), kind=kOutput, calls=%fused_computation.34 | convolution fusion | flops 201457664 | bytes 9699328 | tf_op jit(solution)/shard_map/ftpq,ftdq->ftdp/dot_general | solution.py:96
  560.8 12.1 %copy.184 = f32[16,4,2,8,256]{3,1,0,2,4:T(4,128)} copy(f32[16,4,2,8,256]{4,3,1,0,2:T(8,128)S(1)} %pad_maximum_fusion.1) | data formatting | bytes 2097152
  572.9 22.3 %reshape.151 = f32[256,1024]{1,0:T(8,128)} reshape(f32[256,2,16,4,8]{4,3,2,1,0:T(4,128)} %bitcast.195) | data formatting | bytes 2097152
  596.8 39.7 %psum.48 = f32[]{:T(128)} all-reduce(f32[]{:T(128)} %get-tuple-element.44), channel_id=1, replica_groups=mesh['row'=2,'col'=4,'band'=4] {'row','col','band'}, use_global_device_ids=true, to_apply=%region_10.0 | all-reduce | flops 1 | bytes 8 | tf_op jit(solution)/shard_map/psum | solution.py:92
  666.4 34.3 %all-reduce.9.cloned.1.call-done = f32[4,4096]{1,0:T(4,128)} async-done(((f32[4,4096]{1,0:T(4,128)}), f32[4,4096]{1,0:T(4,128)}) %all-reduce.9.cloned.1.call-update) | async-done | bytes 65552 | tf_op jit(solution)/shard_map/psum | solution.py:71
  (133 shorter events, 143.6 us)
Async XLA Ops:
  8.0 7.9 %copy-start = (f32[4,3,512]{2,0,1:T(4,128)S(1)}, f32[4,3,512]{2,0,1:T(4,128)}, u32[]{:S(2)}) copy-start(f32[4,3,512]{2,0,1:T(4,128)} %param.12) | copy-start | bytes 73732
  8.0 96.6 %all-gather.3.cloned.1.call-start = ((), (), s32[]{:S(2)}) async-start(), calls=%async_computation.2 | async-start | bytes 18874368 | tf_op jit(solution)/shard_map/all_gather | solution.py:77
  11.9 256.6 %all-reduce.5.cloned.1.call-start = ((), (), s32[]{:S(2)}) async-start(), calls=%async_computation.3 | async-start | bytes 131072 | tf_op jit(solution)/shard_map/psum | solution.py:71
  14.9 304.6 %reduce-scatter.7.cloned.1.call-start = ((), (), s32[]{:S(2)}) async-start(), calls=%async_computation.7 | async-start | bytes 1310720
  129.3 31.9 %slice-start = ((s8[8388608]{0:T(1024)(128)(4,1)}), s8[4194304]{0:T(1024)(128)(4,1)S(1)}, s32[]{:S(2)}) async-start(s8[8388608]{0:T(1024)(128)(4,1)} %bitcast.196), calls=%async_computation.9 | async-start | bytes 8388608
  145.2 16.1 %slice-start.1 = ((s8[8388608]{0:T(1024)(128)(4,1)}), s8[4194304]{0:T(1024)(128)(4,1)S(1)}, s32[]{:S(2)}) async-start(s8[8388608]{0:T(1024)(128)(4,1)} %bitcast.196), calls=%async_computation.10 | async-start | bytes 8388608
  241.5 22.5 %copy-start.2 = (f32[16,4,2,8,64]{4,3,2,1,0:T(8,128)S(1)}, f32[16,4,2,8,64]{4,3,2,1,0:T(8,128)}, u32[]{:S(2)}) copy-start(f32[16,4,2,8,64]{4,3,2,1,0:T(8,128)} %param.15) | copy-start | bytes 786436
  241.5 23.2 %copy-start.6 = (f32[16,8]{0,1:T(8,128)S(1)}, f32[16,8]{0,1:T(8,128)}, u32[]{:S(2)}) copy-start(f32[16,8]{0,1:T(8,128)} %param.14) | copy-start | bytes 1540
  241.5 23.7 %copy-start.7 = (f32[3,8]{1,0:T(4,128)S(1)}, f32[3,8]{1,0:T(4,128)}, u32[]{:S(2)}) copy-start(f32[3,8]{1,0:T(4,128)} %param.13) | copy-start | bytes 292
  263.9 170.1 %all-gather.5.cloned.1.call-start = ((), (), s32[]{:S(2)}) async-start(), calls=%async_computation.4 | async-start | bytes 18874368 | tf_op jit(solution)/shard_map/all_gather | solution.py:77
  319.4 18.0 %copy-start.3 = (f32[16,4,2,8,64]{4,3,2,1,0:T(8,128)S(1)}, f32[16,4,2,8,64]{4,3,2,1,0:T(8,128)}, u32[]{:S(2)}) copy-start(f32[16,4,2,8,64]{4,3,2,1,0:T(8,128)} %param.16) | copy-start | bytes 786436
  340.4 101.0 %copy-start.4 = (f32[16,4,2,8,64]{4,0,3,2,1:T(8,128)}, f32[16,4,2,8,64]{4,0,3,2,1:T(8,128)S(1)}, u32[]{:S(2)}) copy-start(f32[16,4,2,8,64]{4,0,3,2,1:T(8,128)S(1)} %get-tuple-element.42) | copy-start | bytes 786436
  343.2 252.1 %all-reduce.7.cloned.1.call-start = ((), (), s32[]{:S(2)}) async-start(), calls=%async_computation.5 | async-start | bytes 131072 | tf_op jit(solution)/shard_map/psum | solution.py:71
  345.8 300.1 %reduce-scatter.9.cloned.1.call-start = ((), (), s32[]{:S(2)}) async-start(), calls=%async_computation.8 | async-start | bytes 1310720
  460.7 31.9 %slice-start.2 = ((s8[8388608]{0:T(1024)(128)(4,1)}), s8[4194304]{0:T(1024)(128)(4,1)S(1)}, s32[]{:S(2)}) async-start(s8[8388608]{0:T(1024)(128)(4,1)} %bitcast.198), calls=%async_computation.11 | async-start | bytes 8388608
  476.6 16.1 %slice-start.3 = ((s8[8388608]{0:T(1024)(128)(4,1)}), s8[4194304]{0:T(1024)(128)(4,1)S(1)}, s32[]{:S(2)}) async-start(s8[8388608]{0:T(1024)(128)(4,1)} %bitcast.198), calls=%async_computation.12 | async-start | bytes 8388608
  595.2 105.5 %all-reduce.9.cloned.1.call-start = ((), (), s32[]{:S(2)}) async-start(), calls=%async_computation.6 | async-start | bytes 131072 | tf_op jit(solution)/shard_map/psum | solution.py:71
  637.9 7.0 copy-start.5
  653.1 50.8 %copy-start.1 = (f32[4,3,512]{2,0,1:T(4,128)S(1)}, f32[4,3,512]{2,0,1:T(4,128)}, u32[]{:S(2)}) copy-start(f32[4,3,512]{2,0,1:T(4,128)} %param.12) | copy-start | bytes 73732
Sparse Core Ops, SparseCore 0:
  12.1 92.4 all-gather.2
  264.0 24.9 reduce-scatter.6
  343.3 90.6 all-gather.4
  595.3 24.7 reduce-scatter.8
Sparse Core Ops, SparseCore 1:
  15.3 36.8 all-reduce.4
  346.0 35.0 all-reduce.6
  665.5 35.1 all-reduce.8
where the time goes:
time: 719 us; the launch traced here: 712 us
  matrix products  215 us (30%)
  waiting for transfers between devices  206 us (29%)
  local copies, waits for them, and re-layouts  163 us (23%)
  blocking collectives  79.8 us (11%)
  other arithmetic  27.9 us (4%)
  between operations  19.3 us (3%)
    all_gather x2, waiting for transfers between devices, shards(): every = lax.all_gather(gain, ('row', 'col'), axis=4, tiled=True)  172 us
    unnamed x48, local copies, waits for them, and re-layouts  124 us
    psum x2, blocking collectives, shards(): lax.psum((jnp.sum(resid_re * resid_re + resid_im * resid_im), jnp.sum(wei...  79.8 us
    dot_general x2, matrix products, shards(): jnp.einsum('ftdp,ftdq->ftpq', row_re, col_im, precision=HIGH)  40.4 us
    dot_general x2, matrix products, shards(): jnp.einsum('ftdp,ftdq->ftpq', row_im, col_im, precision=HIGH)  38.5 us
    psum x3, waiting for transfers between devices, fit(): return solve_fit(lax.psum(rhs, 'band'))  34.3 us
    dot_general x2, matrix products, shards(): jnp.einsum('ftdp,ftdq->ftpq', row_im, col_re, precision=HIGH)  32.1 us
    dot_general x2, matrix products, shards(): jnp.einsum('ftdp,ftdq->ftpq', row_re, col_re, precision=HIGH)  31.7 us
  transfers between devices with their start and end apart: 7, of which 3 were waited for; matrix products, arithmetic and copies ran while one was open for 50% of the time, Pallas kernels for 0%

commit v1 on v0

--- a/solution.py
+++ b/solution.py
@@ -74,7 +74,7 @@
     coeffs = fit(gain, dual)
     for step in range(ITERS):
         target = jnp.einsum("fk,ktcds->ftcds", local_basis, coeffs, precision=HIGH) - dual
-        every = lax.all_gather(gain, ("row", "col"), axis=4, tiled=True)
+        every = jnp.concatenate(lax.all_gather(gain, ("row", "col")), axis=4)
         row_gain = lax.dynamic_slice_in_dim(every, row_start, row_count, 4)
         col_gain = lax.dynamic_slice_in_dim(every, col_start, col_count, 4)
         row_re, row_im = complex_mul(row_gain[:, :, 0], row_gain[:, :, 1], row_cos, row_sin)

time: 719 us -> 572 us (0.80)
  waiting for transfers between devices: 206 us -> 105 us
  local copies, waits for them, and re-layouts: 163 us -> 127 us
  other arithmetic: 27.9 us -> 16.7 us
    all_gather x2, waiting for transfers between devices: 172 us -> 70.4 us  [shards(): every = jnp.concatenate(lax.all_gather(gain, ('row', 'col')), axis=4)]
    unnamed x48 -> x52, local copies, waits for them, and re-layouts: 124 us -> 94.8 us
    slice x4 -> x0, local copies, waits for them, and re-layouts: 23.9 us -> none  [the longest x2 15.4 us: shards(): row_gain[:, :, 0]]
    reshape x0 -> x4, local copies, waits for them, and re-layouts: none -> 18.9 us  [shards(): every = jnp.concatenate(lax.all_gather(gain, ('row', 'col')), axis=4)]
    dot_general x2 -> x0, other arithmetic: 14 us -> none  [shards(): total_mag = jnp.einsum('ftds,fts->ftd', every_mag, all_live, precision=HIGH)]
  transfers between devices with their start and end apart: 7 -> 7, of which waited for: 3 -> 3; matrix products, arithmetic and copies ran while one was open for 50% -> 56% of each run, Pallas kernels for 0% -> 0%
where the time goes in v1:
time: 572 us; the launch traced here: 567 us
  matrix products  219 us (38%)
  local copies, waits for them, and re-layouts  127 us (22%)
  waiting for transfers between devices  105 us (18%)
  blocking collectives  79.7 us (14%)
  between operations  18.7 us (3%)
  other arithmetic  16.7 us (3%)
    unnamed x52, local copies, waits for them, and re-layouts  94.8 us
    psum x2, blocking collectives, shards(): lax.psum((jnp.sum(resid_re * resid_re + resid_im * resid_im), jnp.sum(wei...  79.7 us
    all_gather x2, waiting for transfers between devices, shards(): every = jnp.concatenate(lax.all_gather(gain, ('row', 'col')), axis=4)  70.4 us
    dot_general x2, matrix products, shards(): jnp.einsum('ftdp,ftdq->ftpq', row_re, col_im, precision=HIGH)  40.5 us
    dot_general x2, matrix products, shards(): jnp.einsum('ftdp,ftdq->ftpq', row_im, col_im, precision=HIGH)  38.9 us
    psum x3, waiting for transfers between devices, fit(): return solve_fit(lax.psum(rhs, 'band'))  34.2 us
    dot_general x2, matrix products, shards(): jnp.einsum('ftdp,ftdq->ftpq', row_im, col_re, precision=HIGH)  31.7 us
    dot_general x2, matrix products, shards(): jnp.einsum('ftdp,ftdq->ftpq', row_re, col_re, precision=HIGH)  31.7 us
  transfers between devices with their start and end apart: 7, of which 3 were waited for; matrix products, arithmetic and copies ran while one was open for 56% of the time, Pallas kernels for 0%

profile of v1, /device:TPU:0, one launch (start us, length us, event | category | flops | bytes accessed | tf_op | source)
XLA Modules:
  0.0 566.9 jit_solution(11132306234330278480)
XLA Ops:
  16.3 33.7 %all-gather.5.cloned.1.call-done = f32[128,4,2,8,64]{4,3,2,1,0:T(8,128)} async-done(((f32[16,4,2,8,64]{4,3,2,1,0:T(8,128)}), f32[128,4,2,8,64]{4,3,2,1,0:T(8,128)}) %all-gather.5.cloned.1.call-update) | async-done | bytes 2097168 | tf_op jit(solution)/shard_map/all_gather | solution.py:77
  61.8 15.8 %fusion.124 = f32[16,4,256,128]{3,2,1,0:T(8,128)S(1)} fusion(f32[16,4,8,128]{3,2,1,0:T(8,128)S(1)} %get-tuple-element.20, f32[16,4,2,8,512]{4,3,1,0,2:T(8,128)S(1)} %reshape.148, s32[]{:T(128)S(6)} %select_n.24, s32[]{:T(128)S(6)} %add.260, f32[4,8,256]{2,1,0:T(8,128)S(1)} %convolution_bitcast_fusion, f32[16]{0:T(128)S(1)} %add_multiply_fusion), kind=kOutput, calls=%fused_computation.179 | convolution fusion | flops 201981952 | bytes 9732616 | tf_op jit(solution)/shard_map/ftdp,ftdq->ftpq/dot_general | solution.py:84
  77.7 15.9 %fusion.120 = f32[16,4,256,128]{3,2,1,0:T(8,128)S(1)} fusion(f32[16,4,8,128]{3,2,1,0:T(8,128)S(1)} %get-tuple-element.20, f32[16,4,2,8,512]{4,3,1,0,2:T(8,128)S(1)} %reshape.148, s32[]{:T(128)S(6)} %select_n.24, s32[]{:T(128)S(6)} %add.260, f32[4,8,256]{2,1,0:T(8,128)S(1)} %convolution_bitcast_fusion, f32[16]{0:T(128)S(1)} %add_multiply_fusion), kind=kOutput, calls=%fused_computation.178 | convolution fusion | flops 201981952 | bytes 9732616 | tf_op jit(solution)/shard_map/ftdp,ftdq->ftpq/dot_general | solution.py:87
  93.6 19.5 %fusion = f32[16,4,256,128]{3,2,1,0:T(8,128)S(1)} fusion(f32[16,4,256,128]{3,2,1,0:T(8,128)S(1)} %fusion.124, f32[256,128]{1,0:T(8,128)S(1)} %compare_convert_fusion, f32[16,4,128]{2,1,0:T(4,128)S(1)} %constant_dynamic-slice_fusion.3, f32[16,4,256]{2,1,0:T(4,128)S(1)} %constant_dynamic-slice_fusion.4, bf16[16,4,2,256,128]{4,3,2,1,0:T(8,128)(2,1)S(1)} %bitcast.229, ...), kind=kOutput, calls=%fused_computation.4 | convolution fusion | flops 214564864 | bytes 22544904 | tf_op jit(solution)/shard_map/ftdp,ftdq->ftpq/dot_general | solution.py:84
  113.1 7.2 %fusion.130 = f32[16,4,8,256]{3,2,1,0:T(8,128)S(1)} fusion(f32[16,4,8,128]{3,2,1,0:T(8,128)S(1)} %get-tuple-element.21, f32[16,4,256,128]{3,2,1,0:T(8,128)S(1)} %fusion), kind=kOutput, calls=%fused_computation.183 | convolution fusion | flops 201326592 | bytes 9175040 | tf_op jit(solution)/shard_map/ftpq,ftdq->ftdp/dot_general | solution.py:99
  120.3 7.0 %fusion.129 = f32[16,4,8,256]{3,2,1,0:T(8,128)S(1)} fusion(f32[16,4,8,128]{3,2,1,0:T(8,128)S(1)} %get-tuple-element.20, f32[16,4,256,128]{3,2,1,0:T(8,128)S(1)} %fusion), kind=kOutput, calls=%fused_computation.182 | convolution fusion | flops 201326592 | bytes 9175040 | tf_op jit(solution)/shard_map/ftpq,ftdq->ftdp/dot_general | solution.py:96
  127.3 20.3 %add_reduce_fusion.1 = (f32[]{:T(128)}, f32[16,4,256,128]{3,2,1,0:T(8,128)S(1)}) fusion(f32[16,4,256,128]{3,2,1,0:T(8,128)S(1)} %fusion, f32[16,4,256,128]{3,2,1,0:T(8,128)S(1)} %fusion.120, f32[16,4,8,128]{3,2,1,0:T(8,128)S(1)} %get-tuple-element.21, f32[16,4,2,8,512]{4,3,1,0,2:T(8,128)S(1)} %reshape.148, s32[]{:T(128)S(6)} %select_n.24, s32[]{:T(128)S(6)} %add.260, ...), kind=kOutput, calls=%fused_computation.9 | convolution fusion | flops 222953472 | bytes 30933516 | tf_op jit(solution)/shard_map/ftdp,ftdq->ftpq/dot_general | solution.py:87
  154.6 7.2 %fusion.5 = f32[16,4,1,8,256]{4,3,1,0,2:T(8,128)S(1)} fusion(f32[16,4,8,256]{3,2,1,0:T(8,128)S(1)} %fusion.129, f32[16,4,8,128]{3,2,1,0:T(8,128)S(1)} %get-tuple-element.21, f32[16,4,256,128]{3,2,1,0:T(8,128)S(1)} %get-tuple-element.33), kind=kOutput, calls=%fused_computation.18 | convolution fusion | flops 201457664 | bytes 9699328 | tf_op jit(solution)/shard_map/ftpq,ftdq->ftdp/dot_general | solution.py:96
  161.9 12.0 %copy.110 = f32[16,4,2,8,256]{3,1,0,2,4:T(4,128)} copy(f32[16,4,2,8,256]{4,3,1,0,2:T(8,128)S(1)} %pad_maximum_fusion) | data formatting | bytes 2097152
  174.0 22.3 %reshape.166 = f32[256,1024]{1,0:T(8,128)} reshape(f32[256,2,16,4,8]{4,3,2,1,0:T(4,128)} %bitcast.226) | data formatting | bytes 2097152
  205.1 40.0 %all-reduce = (f32[]{:T(128)}, f32[]{:T(128)}) all-reduce(f32[]{:T(128)} %get-tuple-element.32, f32[]{:T(128)} %fusion.4), channel_id=1, replica_groups=mesh['row'=2,'col'=4,'band'=4] {'row','col','band'}, use_global_device_ids=true, to_apply=%region_2.3 | all-reduce | flops 2 | bytes 16 | tf_op jit(solution)/shard_map/psum | solution.py:92
  250.4 7.2 %reshape.167 = f32[64,2,16,4,8]{4,3,2,1,0:T(4,128)} reshape(f32[64,1024]{1,0:T(8,128)} %reduce-scatter.7.cloned.1.call-done) | data formatting | bytes 524288
  273.5 36.6 %all-gather.7.cloned.1.call-done = f32[128,4,2,8,64]{4,0,3,2,1:T(8,128)} async-done(((f32[16,4,2,8,64]{4,0,3,2,1:T(8,128)}), f32[128,4,2,8,64]{4,0,3,2,1:T(8,128)}) %all-gather.7.cloned.1.call-update) | async-done | bytes 2097168 | tf_op jit(solution)/shard_map/all_gather | solution.py:77
  320.6 15.8 %fusion.118 = f32[16,4,256,128]{3,2,1,0:T(8,128)S(1)} fusion(f32[16,4,8,128]{3,2,1,0:T(8,128)S(1)} %get-tuple-element.19, f32[16,4,2,8,512]{4,3,1,0,2:T(8,128)S(1)} %reshape.152, s32[]{:T(128)S(6)} %select_n.24, s32[]{:T(128)S(6)} %add.260, f32[4,8,256]{2,1,0:T(8,128)S(1)} %convolution_bitcast_fusion, f32[16]{0:T(128)S(1)} %add_multiply_fusion), kind=kOutput, calls=%fused_computation.177 | convolution fusion | flops 201981952 | bytes 9732616 | tf_op jit(solution)/shard_map/ftdp,ftdq->ftpq/dot_general | solution.py:84
  336.5 15.9 %fusion.114 = f32[16,4,256,128]{3,2,1,0:T(8,128)S(1)} fusion(f32[16,4,8,128]{3,2,1,0:T(8,128)S(1)} %get-tuple-element.19, f32[16,4,2,8,512]{4,3,1,0,2:T(8,128)S(1)} %reshape.152, s32[]{:T(128)S(6)} %select_n.24, s32[]{:T(128)S(6)} %add.260, f32[4,8,256]{2,1,0:T(8,128)S(1)} %convolution_bitcast_fusion, f32[16]{0:T(128)S(1)} %add_multiply_fusion), kind=kOutput, calls=%fused_computation.176 | convolution fusion | flops 201981952 | bytes 9732616 | tf_op jit(solution)/shard_map/ftdp,ftdq->ftpq/dot_general | solution.py:87
  352.4 19.5 %fusion.1 = f32[16,4,256,128]{3,2,1,0:T(8,128)S(1)} fusion(f32[16,4,256,128]{3,2,1,0:T(8,128)S(1)} %fusion.118, f32[256,128]{1,0:T(8,128)S(1)} %compare_convert_fusion, f32[16,4,128]{2,1,0:T(4,128)S(1)} %constant_dynamic-slice_fusion.3, f32[16,4,256]{2,1,0:T(4,128)S(1)} %constant_dynamic-slice_fusion.4, bf16[16,4,2,256,128]{4,3,2,1,0:T(8,128)(2,1)S(1)} %bitcast.231, ...), kind=kOutput, calls=%fused_computation.5 | convolution fusion | flops 214564864 | bytes 22544904 | tf_op jit(solution)/shard_map/ftdp,ftdq->ftpq/dot_general | solution.py:84
  371.9 7.2 %fusion.133 = f32[16,4,8,256]{3,2,1,0:T(8,128)S(1)} fusion(f32[16,4,8,128]{3,2,1,0:T(8,128)S(1)} %get-tuple-element.18, f32[16,4,256,128]{3,2,1,0:T(8,128)S(1)} %fusion.1), kind=kOutput, calls=%fused_computation.186 | convolution fusion | flops 201326592 | bytes 9175040 | tf_op jit(solution)/shard_map/ftpq,ftdq->ftdp/dot_general | solution.py:99
  386.1 20.2 %add_reduce_fusion = (f32[]{:T(128)}, f32[16,4,256,128]{3,2,1,0:T(8,128)S(1)}) fusion(f32[16,4,256,128]{3,2,1,0:T(8,128)S(1)} %fusion.1, f32[16,4,256,128]{3,2,1,0:T(8,128)S(1)} %fusion.114, f32[16,4,8,128]{3,2,1,0:T(8,128)S(1)} %get-tuple-element.18, f32[16,4,2,8,512]{4,3,1,0,2:T(8,128)S(1)} %reshape.152, s32[]{:T(128)S(6)} %select_n.24, s32[]{:T(128)S(6)} %add.260, ...), kind=kOutput, calls=%fused_computation.8 | convolution fusion | flops 222953472 | bytes 30933516 | tf_op jit(solution)/shard_map/ftdp,ftdq->ftpq/dot_general | solution.py:87
  413.3 7.2 %fusion.9 = f32[16,4,1,8,256]{4,3,1,0,2:T(8,128)S(1)} fusion(f32[16,4,8,256]{3,2,1,0:T(8,128)S(1)} %fusion.132, f32[16,4,8,128]{3,2,1,0:T(8,128)S(1)} %get-tuple-element.18, f32[16,4,256,128]{3,2,1,0:T(8,128)S(1)} %get-tuple-element.37), kind=kOutput, calls=%fused_computation.22 | convolution fusion | flops 201457664 | bytes 9699328 | tf_op jit(solution)/shard_map/ftpq,ftdq->ftdp/dot_general | solution.py:96
  420.7 12.0 %copy.112 = f32[16,4,2,8,256]{3,1,0,2,4:T(4,128)} copy(f32[16,4,2,8,256]{4,3,1,0,2:T(8,128)S(1)} %pad_maximum_fusion.1) | data formatting | bytes 2097152
  432.7 22.3 %reshape.168 = f32[256,1024]{1,0:T(8,128)} reshape(f32[256,2,16,4,8]{4,3,2,1,0:T(4,128)} %bitcast.227) | data formatting | bytes 2097152
  457.3 39.7 %psum.48 = f32[]{:T(128)} all-reduce(f32[]{:T(128)} %get-tuple-element.36), channel_id=1, replica_groups=mesh['row'=2,'col'=4,'band'=4] {'row','col','band'}, use_global_device_ids=true, to_apply=%region_10.0 | all-reduce | flops 1 | bytes 8 | tf_op jit(solution)/shard_map/psum | solution.py:92
  501.3 7.2 %reshape.169 = f32[64,2,16,4,8]{4,3,2,1,0:T(4,128)} reshape(f32[64,1024]{1,0:T(8,128)} %reduce-scatter.9.cloned.1.call-done) | data formatting | bytes 524288
  521.8 34.2 %all-reduce.9.cloned.1.call-done = f32[4,4096]{1,0:T(4,128)} async-done(((f32[4,4096]{1,0:T(4,128)}), f32[4,4096]{1,0:T(4,128)}) %all-reduce.9.cloned.1.call-update) | async-done | bytes 65552 | tf_op jit(solution)/shard_map/psum | solution.py:71
  (138 shorter events, 102.0 us)
Async XLA Ops:
  8.0 42.0 %all-gather.5.cloned.1.call-start = ((), (), s32[]{:S(2)}) async-start(), calls=%async_computation.5 | async-start | bytes 4718592 | tf_op jit(solution)/shard_map/all_gather | solution.py:77
  8.7 194.2 %all-reduce.5.cloned.1.call-start = ((), (), s32[]{:S(2)}) async-start(), calls=%async_computation.2 | async-start | bytes 131072 | tf_op jit(solution)/shard_map/psum | solution.py:71
  11.7 238.7 %reduce-scatter.7.cloned.1.call-start = ((), (), s32[]{:S(2)}) async-start(), calls=%async_computation.7 | async-start | bytes 1310720
  13.3 36.7 %copy-start.6 = (f32[16,4,512]{2,1,0:T(4,128)}, f32[16,4,512]{2,1,0:T(4,128)S(1)}, u32[]{:S(2)}) copy-start(f32[16,4,512]{2,1,0:T(4,128)S(1)} %get-tuple-element.31) | copy-start | bytes 393220
  15.2 62.5 %copy-start.11 = (f32[4,8,128]{2,1,0:T(8,128)}, f32[4,8,128]{2,1,0:T(8,128)S(1)}, u32[]{:S(2)}) copy-start(f32[4,8,128]{2,1,0:T(8,128)S(1)} %convolution_bitcast_fusion.1) | copy-start | bytes 49156
  61.8 31.7 %slice-start = ((s8[8388608]{0:T(1024)(128)(4,1)}), s8[4194304]{0:T(1024)(128)(4,1)S(1)}, s32[]{:S(2)}) async-start(s8[8388608]{0:T(1024)(128)(4,1)} %bitcast.228), calls=%async_computation.9 | async-start | bytes 8388608
  77.7 15.9 %slice-start.1 = ((s8[8388608]{0:T(1024)(128)(4,1)}), s8[4194304]{0:T(1024)(128)(4,1)S(1)}, s32[]{:S(2)}) async-start(s8[8388608]{0:T(1024)(128)(4,1)} %bitcast.228), calls=%async_computation.10 | async-start | bytes 8388608
  174.0 23.2 %copy-start.2 = (f32[16,4,2,8,64]{4,3,2,1,0:T(8,128)S(1)}, f32[16,4,2,8,64]{4,3,2,1,0:T(8,128)}, u32[]{:S(2)}) copy-start(f32[16,4,2,8,64]{4,3,2,1,0:T(8,128)} %param.15) | copy-start | bytes 786436
  174.0 23.6 %copy-start.13 = (f32[16,8]{0,1:T(8,128)S(1)}, f32[16,8]{0,1:T(8,128)}, u32[]{:S(2)}) copy-start(f32[16,8]{0,1:T(8,128)} %param.14) | copy-start | bytes 1540
  174.0 25.7 %copy-start.14 = (f32[3,8]{1,0:T(4,128)S(1)}, f32[3,8]{1,0:T(4,128)}, u32[]{:S(2)}) copy-start(f32[3,8]{1,0:T(4,128)} %param.13) | copy-start | bytes 292
  196.3 113.9 %all-gather.7.cloned.1.call-start = ((), (), s32[]{:S(2)}) async-start(), calls=%async_computation.6 | async-start | bytes 4718592 | tf_op jit(solution)/shard_map/all_gather | solution.py:77
  199.9 66.7 %copy-start.9 = (f32[4,8,64]{2,1,0:T(8,128)}, f32[4,8,64]{2,1,0:T(8,128)S(1)}, u32[]{:S(2)}) copy-start(f32[4,8,64]{2,1,0:T(8,128)S(1)} %convolution_bitcast_fusion.2) | copy-start | bytes 24580
  250.4 18.3 %copy-start.3 = (f32[16,4,2,8,64]{4,3,2,1,0:T(8,128)S(1)}, f32[16,4,2,8,64]{4,3,2,1,0:T(8,128)}, u32[]{:S(2)}) copy-start(f32[16,4,2,8,64]{4,3,2,1,0:T(8,128)} %param.16) | copy-start | bytes 786436
  271.9 38.2 %copy-start.7 = (f32[16,4,2,8,64]{4,0,3,2,1:T(8,128)}, f32[16,4,2,8,64]{4,0,3,2,1:T(8,128)S(1)}, u32[]{:S(2)}) copy-start(f32[16,4,2,8,64]{4,0,3,2,1:T(8,128)S(1)} %get-tuple-element.35) | copy-start | bytes 786436
  271.9 47.1 %copy-start.12 = (f32[4,8,128]{2,1,0:T(8,128)S(1)}, f32[4,8,128]{2,1,0:T(8,128)}, u32[]{:S(2)}) copy-start(f32[4,8,128]{2,1,0:T(8,128)} %copy-done.11) | copy-start | bytes 49156
  272.0 183.2 %all-reduce.7.cloned.1.call-start = ((), (), s32[]{:S(2)}) async-start(), calls=%async_computation.3 | async-start | bytes 131072 | tf_op jit(solution)/shard_map/psum | solution.py:71
  273.5 227.8 %reduce-scatter.9.cloned.1.call-start = ((), (), s32[]{:S(2)}) async-start(), calls=%async_computation.8 | async-start | bytes 1310720
  320.6 31.7 %slice-start.2 = ((s8[8388608]{0:T(1024)(128)(4,1)}), s8[4194304]{0:T(1024)(128)(4,1)S(1)}, s32[]{:S(2)}) async-start(s8[8388608]{0:T(1024)(128)(4,1)} %bitcast.230), calls=%async_computation.11 | async-start | bytes 8388608
  336.5 15.9 %slice-start.3 = ((s8[8388608]{0:T(1024)(128)(4,1)}), s8[4194304]{0:T(1024)(128)(4,1)S(1)}, s32[]{:S(2)}) async-start(s8[8388608]{0:T(1024)(128)(4,1)} %bitcast.230), calls=%async_computation.12 | async-start | bytes 8388608
  432.7 64.3 %copy-start.8 = (f32[16,4,512,1]{2,1,0,3:T(4,128)S(1)}, f32[16,4,512,1]{2,1,0,3:T(4,128)}, u32[]{:S(2)}) copy-start(f32[16,4,512,1]{2,1,0,3:T(4,128)} %get-tuple-element.30) | copy-start | bytes 393220
  432.7 67.7 %copy-start.5 = (f32[16,4,2,8,64]{4,0,3,2,1:T(8,128)S(1)}, f32[16,4,2,8,64]{4,0,3,2,1:T(8,128)}, u32[]{:S(2)}) copy-start(f32[16,4,2,8,64]{4,0,3,2,1:T(8,128)} %get-tuple-element.34) | copy-start | bytes 786436
  455.1 101.0 %all-reduce.9.cloned.1.call-start = ((), (), s32[]{:S(2)}) async-start(), calls=%async_computation.4 | async-start | bytes 131072 | tf_op jit(solution)/shard_map/psum | solution.py:71
  501.3 16.1 %copy-start.4 = (f32[16,4,2,8,64]{4,3,2,1,0:T(8,128)S(1)}, f32[16,4,2,8,64]{4,3,2,1,0:T(8,128)}, u32[]{:S(2)}) copy-start(f32[16,4,2,8,64]{4,3,2,1,0:T(8,128)} %param.16) | copy-start | bytes 786436
  508.5 50.7 %copy-start.1 = (f32[4,3,512]{2,0,1:T(4,128)S(1)}, f32[4,3,512]{2,0,1:T(4,128)}, u32[]{:S(2)}) copy-start(f32[4,3,512]{2,0,1:T(4,128)} %param.12) | copy-start | bytes 73732
  (2 other events, 20.3 us)
Sparse Core Ops, SparseCore 0:
  10.7 39.2 all-gather.4
  196.4 24.8 reduce-scatter.6
  272.1 38.0 all-gather.6
  455.2 24.8 reduce-scatter.8
Sparse Core Ops, SparseCore 1:
  12.1 36.8 all-reduce.4
  274.8 34.7 all-reduce.6
  520.9 35.0 all-reduce.8
